TPU v7x, 32 devices: a whole 2x2x4 slice. The times are simulated.
32 devices in a mesh: dp: 8 (over y, x, core), tensor: 4 (over z).
Axes of the slice: x: 2, y: 2, z: 4, core: 2. Of those that a mesh axis runs over, the one named last changes fastest.
Arguments:
- tokens: bfloat16 [16384, 768], P(('dp', 'tensor')), may hold values from -6 to 6
- starts: int32 [8, 8], P('dp'), may hold values from 0 to 2047, as said below
- w_qkv: bfloat16 [768, 2304], P(None, 'tensor'), may hold values from -0.21875 to 0.21875
- b_qkv: bfloat16 [2304], P('tensor'), may hold values from -3 to 3
- w_out: bfloat16 [768, 768], P('tensor'), may hold values from -2 to 2
- b_out: bfloat16 [768], replicated, may hold values from -3 to 3
- gain_one: bfloat16 [768], replicated, may hold values from 0.099609375 to 1.8984375
- shift_one: bfloat16 [768], replicated, may hold values from -3 to 3
- w_in: bfloat16 [768, 3072], P(None, 'tensor'), may hold values from -0.21875 to 0.21875
- b_in: bfloat16 [3072], P('tensor'), may hold values from -3 to 3
- w_two: bfloat16 [3072, 768], P('tensor'), may hold values from -0.21875 to 0.21875
- b_two: bfloat16 [768], replicated, may hold values from -3 to 3
- gain_two: bfloat16 [768], replicated, may hold values from 0.099609375 to 1.8984375
- shift_two: bfloat16 [768], replicated, may hold values from -3 to 3
- cotangent: bfloat16 [16384, 768], P(('dp', 'tensor')), may hold values from -6 to 6
Outputs:
- block_out: bfloat16 [16384, 768], P(('dp', 'tensor'))
- d_tokens: bfloat16 [16384, 768], P(('dp', 'tensor'))
- d_w_qkv: float32 [768, 2304], P(None, 'tensor')
- d_b_qkv: float32 [2304], P('tensor')
- d_w_out: float32 [768, 768], P('tensor')
- d_b_out: float32 [768], replicated
- d_gain_one: float32 [768], replicated
- d_shift_one: float32 [768], replicated
- d_w_in: float32 [768, 3072], P(None, 'tensor')
- d_b_in: float32 [3072], P('tensor')
- d_w_two: float32 [3072, 768], P('tensor')
- d_b_two: float32 [768], replicated
- d_gain_two: float32 [768], replicated
- d_shift_two: float32 [768], replicated
Inputs may be any that keep to these rules, and one draw needn't show every extreme that they name: Each row holds exactly 8 documents: its first start is 0 and its starts rise strictly. In the first row the last document is a single token.
All inputs are finite; a program needn't handle non-finite values.
Results may differ from a plain program's by a relative error of at most 0.014.
Values may be sent and summed in bfloat16 or wider, within the bound.
No kernel may reach another device: no remote copies, remote signals or barrier semaphores. Data moves between devices by JAX's collectives and lax.ppermute only.
A program may use at most 192 MiB of HBM per device.

v0:
```python
import math
import jax
import jax.numpy as jnp
from jax import lax
from jax.sharding import PartitionSpec as P

HEAD = 64
GROUP = 64
ROW_LEN = 2048
DOCS = 8
highest = lax.Precision.HIGHEST


def doc_tables(starts_row):
    places = jnp.arange(ROW_LEN, dtype=jnp.int32)
    started = (places[:, None] >= starts_row[None, :]).astype(jnp.int32)
    doc_ids = jnp.sum(started, axis=1) - 1
    onehot = (doc_ids[:, None] == jnp.arange(DOCS, dtype=jnp.int32)[None, :]).astype(jnp.int32)
    finish = jnp.concatenate([starts_row[1:], jnp.full((1,), ROW_LEN, jnp.int32)])
    own_start = jnp.sum(onehot * starts_row[None, :], axis=1)
    own_len = jnp.sum(onehot * (finish - starts_row)[None, :], axis=1)
    angles = 0.5 * math.pi * (places - own_start).astype(jnp.float32) / own_len.astype(jnp.float32)
    return (angles, doc_ids)


def attend(mixed, angles, doc_ids):
    length = mixed.shape[0]
    head_count = mixed.shape[1] // (3 * HEAD)
    blocks = length // GROUP
    pieces = mixed.reshape(blocks, GROUP, head_count, 3, HEAD)
    queries = jax.nn.relu(pieces[:, :, :, 0])
    key_pos = jax.nn.relu(pieces[:, :, :, 1])
    values = pieces[:, :, :, 2]
    cosine = jnp.cos(angles).reshape(blocks, GROUP, 1, 1)
    sines = jnp.sin(angles).reshape(blocks, GROUP, 1, 1)
    query_feat = jnp.concatenate([queries * cosine, queries * sines], axis=-1)
    key_feat = jnp.concatenate([key_pos * cosine, key_pos * sines], axis=-1)
    doc_blocks = doc_ids.reshape(blocks, GROUP)
    within = jnp.arange(GROUP, dtype=jnp.int32)
    inside_mask = (
        (doc_blocks[:, :, None] == doc_blocks[:, None, :])
        & (within[None, :, None] >= within[None, None, :])
    ).astype(jnp.float32)
    scores = (
        jnp.einsum("bihf,bjhf->bhij", query_feat, key_feat, precision=highest)
        * inside_mask[:, None]
    )
    numerator = jnp.einsum("bhij,bjhd->bihd", scores, values, precision=highest)
    denominator = jnp.transpose(jnp.sum(scores, axis=-1), (0, 2, 1))
    first_doc = doc_blocks[:, 0]
    last_doc = doc_blocks[:, -1]
    tail_mask = (doc_blocks == last_doc[:, None]).astype(jnp.float32)
    states = jnp.einsum("bjhf,bjhd,bj->bhfd", key_feat, values, tail_mask, precision=highest)
    key_sums = jnp.einsum("bjhf,bj->bhf", key_feat, tail_mask, precision=highest)
    order = jnp.arange(blocks, dtype=jnp.int32)
    link_mask = (
        (last_doc[None, :] == first_doc[:, None]) & (order[None, :] < order[:, None])
    ).astype(jnp.float32)
    carried = jnp.einsum("cb,bhfd->chfd", link_mask, states, precision=highest)
    carried_sum = jnp.einsum("cb,bhf->chf", link_mask, key_sums, precision=highest)
    opening = (doc_blocks == first_doc[:, None]).astype(jnp.float32)
    numerator = numerator + jnp.einsum(
        "bihf,bhfd,bi->bihd", query_feat, carried, opening, precision=highest
    )
    denominator = denominator + jnp.einsum(
        "bihf,bhf,bi->bih", query_feat, carried_sum, opening, precision=highest
    )
    result = numerator / jnp.maximum(denominator, 1.0)[..., None]
    return result.reshape(length, head_count * HEAD)


def attend_rows(mixed, angles, doc_ids):
    row_count = angles.shape[0]
    shaped = mixed.reshape(row_count, angles.shape[1], mixed.shape[1])
    return jax.vmap(attend)(shaped, angles, doc_ids).reshape(mixed.shape[0], -1)


def normalize(rows_in, gain, shift):
    centred = rows_in - jnp.mean(rows_in, axis=-1, keepdims=True)
    spread = jnp.mean(centred * centred, axis=-1, keepdims=True)
    return centred * lax.rsqrt(spread + 1e-05) * gain + shift


def smooth(values):
    return jax.nn.gelu(values)


def inner_rows(left, right):
    return lax.dot_general(
        left, right, (((0,), (0,)), ((), ())), preferred_element_type=jnp.float32
    )


def times_rows(left, right):
    return lax.dot_general(
        left, right, (((1,), (1,)), ((), ())), preferred_element_type=jnp.float32
    )


def rows_product(source, weight):
    return jnp.dot(source, weight, preferred_element_type=jnp.float32)


def rows_back(source, weight):
    return times_rows(source, weight)


def on_device(
    tokens,
    starts,
    w_qkv,
    b_qkv,
    w_out,
    b_out,
    gain_one,
    shift_one,
    w_in,
    b_in,
    w_two,
    b_two,
    gain_two,
    shift_two,
    cotangent,
):
    angles, doc_ids = jax.vmap(doc_tables)(starts)
    bias_qkv = b_qkv.astype(jnp.float32)
    bias_in = b_in.astype(jnp.float32)
    gain_a = gain_one.astype(jnp.float32)
    shift_a = shift_one.astype(jnp.float32)
    gain_b = gain_two.astype(jnp.float32)
    shift_b = shift_two.astype(jnp.float32)
    input_full = lax.all_gather(tokens, "tensor", axis=0, tiled=True)
    mixed = jnp.dot(input_full, w_qkv, preferred_element_type=jnp.float32) + bias_qkv
    attended = attend_rows(mixed, angles, doc_ids).astype(jnp.bfloat16)
    branch = lax.psum_scatter(
        rows_product(attended, w_out), "tensor", scatter_dimension=0, tiled=True
    ) + b_out.astype(jnp.float32)
    first_sum = tokens.astype(jnp.float32) + branch
    first_low = normalize(first_sum, gain_a, shift_a).astype(jnp.bfloat16)
    middle_full = lax.all_gather(first_low, "tensor", axis=0, tiled=True)
    hidden = jnp.dot(middle_full, w_in, preferred_element_type=jnp.float32) + bias_in
    active = smooth(hidden).astype(jnp.bfloat16)
    second = lax.psum_scatter(
        rows_product(active, w_two), "tensor", scatter_dimension=0, tiled=True
    ) + b_two.astype(jnp.float32)
    second_sum = first_low.astype(jnp.float32) + second
    block_out = normalize(second_sum, gain_b, shift_b).astype(jnp.bfloat16)
    input_back = lax.all_gather(tokens, "tensor", axis=0, tiled=True)
    middle_back = lax.all_gather(first_low, "tensor", axis=0, tiled=True)
    unused_two, norm_two_back = jax.vjp(normalize, second_sum, gain_b, shift_b)
    d_r2, d_gain_two, d_shift_two = norm_two_back(cotangent.astype(jnp.float32))
    d_second = d_r2.astype(jnp.bfloat16)
    d_b_two = jnp.sum(d_second, axis=0, dtype=jnp.float32)
    second_full = lax.all_gather(d_second, "tensor", axis=0, tiled=True)
    hidden_again = jnp.dot(middle_back, w_in, preferred_element_type=jnp.float32) + bias_in
    active_val, gelu_back = jax.vjp(smooth, hidden_again)
    active_again = active_val.astype(jnp.bfloat16)
    d_w_two = inner_rows(active_again, second_full)
    d_active = times_rows(second_full, w_two)
    d_hidden = gelu_back(d_active)[0].astype(jnp.bfloat16)
    d_b_in = jnp.sum(d_hidden, axis=0, dtype=jnp.float32)
    d_w_in = inner_rows(middle_back, d_hidden)
    d_first = (
        lax.psum_scatter(rows_back(d_hidden, w_in), "tensor", scatter_dimension=0, tiled=True)
        + d_r2
    )
    unused_one, norm_one_back = jax.vjp(normalize, first_sum, gain_a, shift_a)
    d_r1, d_gain_one, d_shift_one = norm_one_back(d_first)
    d_branch = d_r1.astype(jnp.bfloat16)
    d_b_out = jnp.sum(d_branch, axis=0, dtype=jnp.float32)
    branch_full = lax.all_gather(d_branch, "tensor", axis=0, tiled=True)
    mixed_again = jnp.dot(input_back, w_qkv, preferred_element_type=jnp.float32) + bias_qkv
    attended_val, attend_back = jax.vjp(
        lambda mixed_in: attend_rows(mixed_in, angles, doc_ids), mixed_again
    )
    attended_again = attended_val.astype(jnp.bfloat16)
    d_w_out = inner_rows(attended_again, branch_full)
    d_attended = times_rows(branch_full, w_out)
    d_mixed = attend_back(d_attended)[0].astype(jnp.bfloat16)
    d_b_qkv = jnp.sum(d_mixed, axis=0, dtype=jnp.float32)
    d_w_qkv = inner_rows(input_back, d_mixed)
    d_tokens = (
        lax.psum_scatter(
            rows_back(d_mixed, w_qkv).astype(jnp.bfloat16),
            "tensor",
            scatter_dimension=0,
            tiled=True,
        ).astype(jnp.float32)
        + d_r1
    ).astype(jnp.bfloat16)
    d_w_qkv, d_b_qkv, d_w_out, d_w_in, d_b_in, d_w_two = lax.psum(
        (d_w_qkv, d_b_qkv, d_w_out, d_w_in, d_b_in, d_w_two), "dp"
    )
    d_b_out, d_gain_one, d_shift_one, d_b_two, d_gain_two, d_shift_two = lax.psum(
        (d_b_out, d_gain_one, d_shift_one, d_b_two, d_gain_two, d_shift_two), ("dp", "tensor")
    )
    return (
        block_out,
        d_tokens,
        d_w_qkv,
        d_b_qkv,
        d_w_out,
        d_b_out,
        d_gain_one,
        d_shift_one,
        d_w_in,
        d_b_in,
        d_w_two,
        d_b_two,
        d_gain_two,
        d_shift_two,
    )


def solution(mesh):
    in_specs = (
        P(("dp", "tensor"), None),
        P("dp", None),
        P(None, "tensor"),
        P("tensor"),
        P("tensor", None),
        P(),
        P(),
        P(),
        P(None, "tensor"),
        P("tensor"),
        P("tensor", None),
        P(),
        P(),
        P(),
        P(("dp", "tensor"), None),
    )
    out_specs = (
        P(("dp", "tensor"), None),
        P(("dp", "tensor"), None),
        P(None, "tensor"),
        P("tensor"),
        P("tensor", None),
        P(),
        P(),
        P(),
        P(None, "tensor"),
        P("tensor"),
        P("tensor", None),
        P(),
        P(),
        P(),
    )
    return jax.shard_map(
        on_device, mesh=mesh, in_specs=in_specs, out_specs=out_specs, check_vma=False
    )
```

profile of v0, /device:TPU:0, one launch (start us, length us, event | category | flops | bytes accessed | tf_op | source)
XLA Modules:
  0.0 1038.7 jit_solution(10530214980209661449)
XLA Ops:
  12.7 63.1 %all-gather.5.cloned.1.call-done = bf16[2048,768]{1,0:T(8,128)(2,1)} async-done(((bf16[512,768]{1,0:T(8,128)(2,1)}), bf16[2048,768]{1,0:T(8,128)(2,1)}) %all-gather.5.cloned.1.call-update) | async-done | bytes 3145744 | tf_op jit(solution)/shard_map/all_gather | solution.py:132
  82.2 8.7 reshape_reshape.3
  90.9 8.2 fusion.101
  150.5 9.1 divide_convert_fusion
  169.7 107.1 %reduce-scatter.5.cloned.1.call-done = f32[512,768]{1,0:T(8,128)} async-done(((f32[2048,768]{1,0:T(8,128)}), f32[512,768]{1,0:T(8,128)}) %reduce-scatter.5.cloned.1.call-update) | async-done | bytes 1572880 | tf_op jit(solution)/shard_map/reduce_scatter | solution.py:135
  280.2 64.1 %all-gather.7.cloned.1.call-done = bf16[2048,768]{1,0:T(8,128)(2,1)} async-done(((bf16[512,768]{1,0:T(8,128)(2,1)}), bf16[2048,768]{1,0:T(8,128)(2,1)}) %all-gather.7.cloned.1.call-update) | async-done | bytes 3145744 | tf_op jit(solution)/shard_map/all_gather | solution.py:140
  344.3 8.4 multiply_convert_fusion
  361.3 107.1 %reduce-scatter.7.cloned.1.call-done = f32[512,768]{1,0:T(8,128)} async-done(((f32[2048,768]{1,0:T(8,128)}), f32[512,768]{1,0:T(8,128)}) %reduce-scatter.7.cloned.1.call-update) | async-done | bytes 1572880 | tf_op jit(solution)/shard_map/reduce_scatter | solution.py:143
  476.5 64.1 %all-gather.9.cloned.1.call-done = bf16[2048,768]{1,0:T(8,128)(2,1)} async-done(((bf16[512,768]{1,0:T(8,128)(2,1)}), bf16[2048,768]{1,0:T(8,128)(2,1)}) %all-gather.9.cloned.1.call-update) | async-done | bytes 3145744 | tf_op jit(solution)/shard_map/all_gather | solution.py:154
  540.6 9.8 convert_reduce_fusion.1
  556.7 109.5 %reduce-scatter.9.cloned.1.call-done = f32[512,768]{1,0:T(8,128)} async-done(((f32[2048,768]{1,0:T(8,128)}), f32[512,768]{1,0:T(8,128)}) %reduce-scatter.9.cloned.1.call-update) | async-done | bytes 1572880 | tf_op jit(solution)/shard_map/reduce_scatter | solution.py:164
  673.7 63.5 %all-gather.11.cloned.1.call-done = bf16[2048,768]{1,0:T(8,128)(2,1)} async-done(((bf16[512,768]{1,0:T(8,128)(2,1)}), bf16[2048,768]{1,0:T(8,128)(2,1)}) %all-gather.11.cloned.1.call-update) | async-done | bytes 3145744 | tf_op jit(solution)/shard_map/all_gather | solution.py:171
  742.9 12.0 %fusion.21 = f32[32,3,64,64]{2,3,1,0:T(8,128)} fusion(f32[32,3,64,64]{2,3,1,0:T(8,128)} %copy-done.21, f32[32,64,64]{1,2,0:T(8,128)S(1)} %copy-done.12, f32[1,32,64,3,64]{2,1,4,3,0:T(8,128)} %reshape.798, f32[32,64,3]{1,2,0:T(4,128)S(1)} %copy-done.42), kind=kOutput, calls=%fused_computation.38 | convolution fusion | flops 302776320 | bytes 5267456 | tf_op jit(solution)/shard_map/transpose(jvp(vmap(bhij,bjhd->bihd)))/dot_general | solution.py:48
  754.9 7.4 fusion.19
  777.2 8.3 fusion.42
  795.2 7.7 fusion.13
  802.9 7.0 fusion.38
  814.7 8.1 add_bitcast_fusion
  828.5 7.4 copy.171
  835.9 6.7 convert_element_type.170
  847.0 7.1 fusion.108
  864.5 43.0 %all-reduce.3 = (f32[768]{0:T(1024)}, f32[768]{0:T(1024)}, f32[768]{0:T(1024)}, f32[768]{0:T(1024)}, f32[768]{0:T(1024)}, /*index=5*/f32[768]{0:T(1024)}) all-reduce(f32[768]{0:T(1024)S(1)} %copy-done.71, f32[768]{0:T(1024)S(1)} %copy-done.72, f32[768]{0:T(1024)S(1)} %copy-done.73, ...), channel_id=1, replica_groups=mesh['dp'=8,'tensor'=4] {'dp','tensor'}, use_global_device_ids=true, to_apply=%region_22.23 | all-reduce | flops 4608 | bytes 36864 | tf_op jit(solution)/shard_map/psum | solution.py:194
  907.5 14.0 %all-reduce.4 = (f32[576]{0:T(1024)}, f32[768]{0:T(1024)}) all-reduce(f32[576]{0:T(1024)S(1)} %reduce_sum.223, f32[768]{0:T(1024)S(1)} %copy-done.76), channel_id=1, replica_groups=mesh['dp'=8,'tensor'=4] {'dp'}, use_global_device_ids=true, to_apply=%region_19.20 | all-reduce | flops 1344 | bytes 10752 | tf_op jit(solution)/shard_map/psum | solution.py:191
  923.8 101.3 %all-reduce.8.cloned.1.call-done = (f32[768,576]{0,1:T(8,128)}, f32[192,768]{1,0:T(8,128)}, f32[768,768]{1,0:T(8,128)}, f32[768,768]{1,0:T(8,128)}) async-done(((f32[768,576]{0,1:T(8,128)}, f32[192,768]{1,0:T(8,128)}, f32[768,768]{1,0:T(8,128)}, f32[768,768]{1,0:T(8,128)}), (f32[768,576]{0,1:T(8,128)}, f32[192,768]{1,0:T(8,128)}, f32[768,768]{1,0:T(8,128)}, ...) | async-done | bytes 7077904 | tf_op jit(solution)/shard_map/psum | solution.py:191
  (289 shorter events, 170.7 us)
Async XLA Ops:
  7.2 337.2 %copy-start = (bf16[768,768]{1,0:T(8,128)(2,1)S(1)}, bf16[768,768]{1,0:T(8,128)(2,1)}, u32[]{:S(2)}) copy-start(bf16[768,768]{1,0:T(8,128)(2,1)} %param.23) | copy-start | bytes 3538948
  7.2 68.6 %all-gather.5.cloned.1.call-start = ((), (), s32[]{:S(2)}) async-start(), calls=%async_computation.4 | async-start | bytes 3932160 | tf_op jit(solution)/shard_map/all_gather | solution.py:132
  7.9 268.9 %reduce-scatter.5.cloned.1.call-start = ((), (), s32[]{:S(2)}) async-start(), calls=%async_computation.5 | async-start | bytes 7864320 | tf_op jit(solution)/shard_map/reduce_scatter | solution.py:135
  12.1 117.7 %copy-start.61 = (s32[32]{0:T(128)}, s32[32]{0:T(128)S(1)}, u32[]{:S(2)}) copy-start(s32[32]{0:T(128)S(1)} %get-tuple-element.20) | copy-start | bytes 388
  12.1 117.7 %copy-start.64 = (s32[32]{0:T(128)}, s32[32]{0:T(128)S(1)}, u32[]{:S(2)}) copy-start(s32[32]{0:T(128)S(1)} %get-tuple-element.21) | copy-start | bytes 388
  12.2 109.0 %copy-start.39 = (f32[32,64]{1,0:T(8,128)}, f32[32,64]{1,0:T(8,128)S(1)}, u32[]{:S(2)}) copy-start(f32[32,64]{1,0:T(8,128)S(1)} %get-tuple-element.57) | copy-start | bytes 24580
  12.3 98.5 %copy-start.44 = (f32[32,64]{1,0:T(8,128)}, f32[32,64]{1,0:T(8,128)S(1)}, u32[]{:S(2)}) copy-start(f32[32,64]{1,0:T(8,128)S(1)} %get-tuple-element.71) | copy-start | bytes 24580
  12.3 98.4 %copy-start.46 = (f32[32,64]{1,0:T(8,128)}, f32[32,64]{1,0:T(8,128)S(1)}, u32[]{:S(2)}) copy-start(f32[32,64]{1,0:T(8,128)S(1)} %get-tuple-element.72) | copy-start | bytes 24580
  12.7 131.7 %copy-start.11 = (f32[32,64,64]{1,2,0:T(8,128)}, f32[32,64,64]{1,2,0:T(8,128)S(1)}, u32[]{:S(2)}) copy-start(f32[32,64,64]{1,2,0:T(8,128)S(1)} %and_convert_fusion) | copy-start | bytes 1572868
  167.2 109.6 %copy-start.27 = (bf16[512,768]{1,0:T(8,128)(2,1)S(1)}, bf16[512,768]{1,0:T(8,128)(2,1)}, u32[]{:S(2)}) copy-start(bf16[512,768]{1,0:T(8,128)(2,1)} %param.15) | copy-start | bytes 2359300
  167.3 177.1 %all-gather.7.cloned.1.call-start = ((), (), s32[]{:S(2)}) async-start(), calls=%async_computation.6 | async-start | bytes 3932160 | tf_op jit(solution)/shard_map/all_gather | solution.py:140
  278.6 74.1 %copy-start.50 = (f32[512]{0:T(512)}, f32[512]{0:T(512)S(1)}, u32[]{:S(2)}) copy-start(f32[512]{0:T(512)S(1)} %broadcast_multiply_fusion.1) | copy-start | bytes 6148
  278.9 73.8 %copy-start.57 = (f32[512]{0:T(512)}, f32[512]{0:T(512)S(1)}, u32[]{:S(2)}) copy-start(f32[512]{0:T(512)S(1)} %multiply_reduce_fusion.5) | copy-start | bytes 6148
  280.2 188.3 %reduce-scatter.7.cloned.1.call-start = ((), (), s32[]{:S(2)}) async-start(), calls=%async_computation.7 | async-start | bytes 7864320 | tf_op jit(solution)/shard_map/reduce_scatter | solution.py:143
  358.9 181.8 %all-gather.9.cloned.1.call-start = ((), (), s32[]{:S(2)}) async-start(), calls=%async_computation.8 | async-start | bytes 3932160 | tf_op jit(solution)/shard_map/all_gather | solution.py:154
  361.3 109.5 %copy-start.26 = (bf16[512,768]{1,0:T(8,128)(2,1)S(1)}, bf16[512,768]{1,0:T(8,128)(2,1)}, u32[]{:S(2)}) copy-start(bf16[512,768]{1,0:T(8,128)(2,1)} %param.29) | copy-start | bytes 2359300
  476.4 189.7 %reduce-scatter.9.cloned.1.call-start = ((), (), s32[]{:S(2)}) async-start(), calls=%async_computation.9 | async-start | bytes 7864320 | tf_op jit(solution)/shard_map/reduce_scatter | solution.py:164
  556.6 109.6 %copy-start.49 = (f32[768]{0:T(1024)S(1)}, f32[768]{0:T(1024)}, u32[]{:S(2)}) copy-start(f32[768]{0:T(1024)} %convert_element_type.155) | copy-start | bytes 9220
  556.6 109.6 %copy-start.51 = (f32[512]{0:T(512)S(1)}, f32[512]{0:T(512)}, u32[]{:S(2)}) copy-start(f32[512]{0:T(512)} %copy-done.50) | copy-start | bytes 6148
  556.6 109.6 %copy-start.54 = (f32[512]{0:T(512)S(1)}, f32[512]{0:T(512)}, u32[]{:S(2)}) copy-start(f32[512]{0:T(512)} %copy-done.53) | copy-start | bytes 6148
  556.6 112.9 %copy-start.58 = (f32[512]{0:T(512)S(1)}, f32[512]{0:T(512)}, u32[]{:S(2)}) copy-start(f32[512]{0:T(512)} %copy-done.57) | copy-start | bytes 6148
  556.6 180.5 %all-gather.11.cloned.1.call-start = ((), (), s32[]{:S(2)}) async-start(), calls=%async_computation.10 | async-start | bytes 3932160 | tf_op jit(solution)/shard_map/all_gather | solution.py:171
  673.0 248.5 %reduce-scatter.11.cloned.1.call-start = ((), (), s32[]{:S(2)}) async-start(), calls=%async_computation.11 | async-start | bytes 3932160 | tf_op jit(solution)/shard_map/reduce_scatter | solution.py:183
  846.7 178.4 %all-reduce.8.cloned.1.call-start = ((), (), s32[]{:S(2)}) async-start(), calls=%async_computation.12 | async-start | bytes 14155776 | tf_op jit(solution)/shard_map/psum | solution.py:191
  (76 other events, 865.4 us)
Sparse Core Ops, SparseCore 0:
  9.6 66.1 all-gather.4
  167.4 109.3 reduce-scatter.4
  280.3 64.0 all-gather.6
  359.0 109.3 reduce-scatter.6
  476.6 64.0 all-gather.8
  556.7 109.3 reduce-scatter.8
  673.1 64.0 all-gather.10
  846.8 59.8 reduce-scatter.10
  911.5 113.5 all-reduce.7
where the time goes:
time: 1050 us; the launch traced here: 1040 us
  waiting for transfers between devices  681 us (65%)
  matrix products  166 us (16%)
  local copies, waits for them, and re-layouts  73.7 us (7%)
  blocking collectives  57 us (5%)
  other arithmetic  45.5 us (4%)
  between operations  15.3 us (1%)
    reduce_scatter x1, waiting for transfers between devices, on_device(): lax.psum_scatter(rows_back(d_hidden, w_in), 'tensor', scatter_dimension=0...  109 us
    reduce_scatter x1, waiting for transfers between devices, on_device(): lax.psum_scatter(rows_product(attended, w_out), 'tensor', scatter_dimensi...  107 us
    reduce_scatter x1, waiting for transfers between devices, on_device(): lax.psum_scatter(rows_product(active, w_two), 'tensor', scatter_dimension...  107 us
    psum x1, waiting for transfers between devices, on_device(): lax.psum((d_w_qkv, d_b_qkv, d_w_out, d_w_in, d_b_in, d_w_two), 'dp')  101 us
    all_gather x1, waiting for transfers between devices, on_device(): second_full = lax.all_gather(d_second, 'tensor', axis=0, tiled=True)  64.1 us
    all_gather x1, waiting for transfers between devices, on_device(): middle_full = lax.all_gather(first_low, 'tensor', axis=0, tiled=True)  64.1 us
    all_gather x1, waiting for transfers between devices, on_device(): branch_full = lax.all_gather(d_branch, 'tensor', axis=0, tiled=True)  63.5 us
    all_gather x1, waiting for transfers between devices, on_device(): input_full = lax.all_gather(tokens, 'tensor', axis=0, tiled=True)  63.1 us
  transfers between devices with their start and end apart: 9, of which 8 were waited for; matrix products, arithmetic and copies ran while one was open for 3% of the time, Pallas kernels for 0%

commit v1 on v0

--- a/solution.py
+++ b/solution.py
@@ -1,3 +1,4 @@
+import functools
 import math
 import jax
 import jax.numpy as jnp
@@ -9,6 +10,15 @@
 ROW_LEN = 2048
 DOCS = 8
 highest = lax.Precision.HIGHEST
+
+
+def wrap_pipes(message, axis_id, mesh_name):
+    for i0 in (axis_id, mesh_name):
+        message = lax.psum(message, i0)
+    return message
+
+
+write_domain_by_axis = functools.partial(wrap_pipes, axis_id="tensor", mesh_name="dp")
 
 
 def doc_tables(starts_row):
@@ -191,8 +201,8 @@
     d_w_qkv, d_b_qkv, d_w_out, d_w_in, d_b_in, d_w_two = lax.psum(
         (d_w_qkv, d_b_qkv, d_w_out, d_w_in, d_b_in, d_w_two), "dp"
     )
-    d_b_out, d_gain_one, d_shift_one, d_b_two, d_gain_two, d_shift_two = lax.psum(
-        (d_b_out, d_gain_one, d_shift_one, d_b_two, d_gain_two, d_shift_two), ("dp", "tensor")
+    d_b_out, d_gain_one, d_shift_one, d_b_two, d_gain_two, d_shift_two = write_domain_by_axis(
+        (d_b_out, d_gain_one, d_shift_one, d_b_two, d_gain_two, d_shift_two)
     )
     return (
         block_out,

time: 1050 us -> 1040 us (level)
  blocking collectives: 57 us -> 43.7 us
  waiting for transfers between devices: 681 us -> 694 us
    psum x1, blocking collectives: 43 us -> 19.9 us  [wrap_pipes(): message = lax.psum(message, i0)]
    psum x1, waiting for transfers between devices: 101 us -> 115 us  [on_device(): lax.psum((d_w_qkv, d_b_qkv, d_w_out, d_w_in, d_b_in, d_w_two), 'dp')]
where the time goes in v1:
time: 1040 us
  waiting for transfers between devices  694 us (67%)
  matrix products  166 us (16%)
  local copies, waits for them, and re-layouts  73.7 us (7%)
  other arithmetic  45.5 us (4%)
  blocking collectives  43.7 us (4%)
  between operations  15.3 us (1%)
    psum x1, waiting for transfers between devices, on_device(): lax.psum((d_w_qkv, d_b_qkv, d_w_out, d_w_in, d_b_in, d_w_two), 'dp')  115 us
    reduce_scatter x1, waiting for transfers between devices, on_device(): lax.psum_scatter(rows_back(d_hidden, w_in), 'tensor', scatter_dimension=0...  109 us
    reduce_scatter x1, waiting for transfers between devices, on_device(): lax.psum_scatter(rows_product(attended, w_out), 'tensor', scatter_dimensi...  107 us
    reduce_scatter x1, waiting for transfers between devices, on_device(): lax.psum_scatter(rows_product(active, w_two), 'tensor', scatter_dimension...  107 us
    all_gather x1, waiting for transfers between devices, on_device(): second_full = lax.all_gather(d_second, 'tensor', axis=0, tiled=True)  64.1 us
    all_gather x1, waiting for transfers between devices, on_device(): middle_full = lax.all_gather(first_low, 'tensor', axis=0, tiled=True)  64.1 us
    all_gather x1, waiting for transfers between devices, on_device(): branch_full = lax.all_gather(d_branch, 'tensor', axis=0, tiled=True)  63.5 us
    all_gather x1, waiting for transfers between devices, on_device(): input_full = lax.all_gather(tokens, 'tensor', axis=0, tiled=True)  63.1 us
  transfers between devices with their start and end apart: 9, of which 8 were waited for; matrix products, arithmetic and copies ran while one was open for 3% of the time, Pallas kernels for 0%

profile of v1, /device:TPU:0, one launch (start us, length us, event | category | flops | bytes accessed | tf_op | source)
XLA Modules:
  0.0 1038.6 jit_solution(8130398211555783654)
XLA Ops:
  12.7 63.1 %all-gather.5.cloned.1.call-done = bf16[2048,768]{1,0:T(8,128)(2,1)} async-done(((bf16[512,768]{1,0:T(8,128)(2,1)}), bf16[2048,768]{1,0:T(8,128)(2,1)}) %all-gather.5.cloned.1.call-update) | async-done | bytes 3145744 | tf_op jit(solution)/shard_map/all_gather | solution.py:142
  82.2 8.7 reshape_reshape.3
  90.9 8.2 fusion.101
  150.5 9.1 divide_convert_fusion
  169.7 107.1 %reduce-scatter.5.cloned.1.call-done = f32[512,768]{1,0:T(8,128)} async-done(((f32[2048,768]{1,0:T(8,128)}), f32[512,768]{1,0:T(8,128)}) %reduce-scatter.5.cloned.1.call-update) | async-done | bytes 1572880 | tf_op jit(solution)/shard_map/reduce_scatter | solution.py:145
  280.2 64.1 %all-gather.7.cloned.1.call-done = bf16[2048,768]{1,0:T(8,128)(2,1)} async-done(((bf16[512,768]{1,0:T(8,128)(2,1)}), bf16[2048,768]{1,0:T(8,128)(2,1)}) %all-gather.7.cloned.1.call-update) | async-done | bytes 3145744 | tf_op jit(solution)/shard_map/all_gather | solution.py:150
  344.3 8.4 multiply_convert_fusion
  361.3 107.1 %reduce-scatter.7.cloned.1.call-done = f32[512,768]{1,0:T(8,128)} async-done(((f32[2048,768]{1,0:T(8,128)}), f32[512,768]{1,0:T(8,128)}) %reduce-scatter.7.cloned.1.call-update) | async-done | bytes 1572880 | tf_op jit(solution)/shard_map/reduce_scatter | solution.py:153
  476.5 64.1 %all-gather.9.cloned.1.call-done = bf16[2048,768]{1,0:T(8,128)(2,1)} async-done(((bf16[512,768]{1,0:T(8,128)(2,1)}), bf16[2048,768]{1,0:T(8,128)(2,1)}) %all-gather.9.cloned.1.call-update) | async-done | bytes 3145744 | tf_op jit(solution)/shard_map/all_gather | solution.py:164
  540.6 9.8 convert_reduce_fusion.1
  556.6 109.5 %reduce-scatter.9.cloned.1.call-done = f32[512,768]{1,0:T(8,128)} async-done(((f32[2048,768]{1,0:T(8,128)}), f32[512,768]{1,0:T(8,128)}) %reduce-scatter.9.cloned.1.call-update) | async-done | bytes 1572880 | tf_op jit(solution)/shard_map/reduce_scatter | solution.py:174
  673.7 63.5 %all-gather.11.cloned.1.call-done = bf16[2048,768]{1,0:T(8,128)(2,1)} async-done(((bf16[512,768]{1,0:T(8,128)(2,1)}), bf16[2048,768]{1,0:T(8,128)(2,1)}) %all-gather.11.cloned.1.call-update) | async-done | bytes 3145744 | tf_op jit(solution)/shard_map/all_gather | solution.py:181
  742.9 12.0 %fusion.21 = f32[32,3,64,64]{2,3,1,0:T(8,128)} fusion(f32[32,3,64,64]{2,3,1,0:T(8,128)} %copy-done.21, f32[32,64,64]{1,2,0:T(8,128)S(1)} %copy-done.12, f32[1,32,64,3,64]{2,1,4,3,0:T(8,128)} %reshape.798, f32[32,64,3]{1,2,0:T(4,128)S(1)} %copy-done.42), kind=kOutput, calls=%fused_computation.38 | convolution fusion | flops 302776320 | bytes 5267456 | tf_op jit(solution)/shard_map/transpose(jvp(vmap(bhij,bjhd->bihd)))/dot_general | solution.py:58
  754.8 7.4 fusion.19
  777.2 8.3 fusion.42
  795.1 7.7 fusion.13
  802.9 7.0 fusion.38
  814.7 8.1 add_bitcast_fusion
  828.5 7.3 copy.171
  835.8 6.7 convert_element_type.170
  846.9 7.1 fusion.108
  864.4 19.9 %all-reduce.5 = (f32[768]{0:T(1024)S(1)}, f32[768]{0:T(1024)S(1)}, f32[768]{0:T(1024)S(1)}, f32[768]{0:T(1024)S(1)}, f32[768]{0:T(1024)S(1)}, /*index=5*/f32[768]{0:T(1024)S(1)}) all-reduce(f32[768]{0:T(1024)S(1)} %copy-done.71, f32[768]{0:T(1024)S(1)} %copy-done.72, ...), channel_id=1, replica_groups=mesh['dp'=8,'tensor'=4] {'tensor'}, use_global_device_ids=true, to_apply=%region_22.23 | all-reduce | flops 4608 | bytes 36864 | tf_op jit(solution)/shard_map/psum | solution.py:17
  884.4 23.8 %all-reduce.3 = (f32[576]{0:T(1024)}, f32[768]{0:T(1024)}, f32[768]{0:T(1024)}, f32[768]{0:T(1024)}, f32[768]{0:T(1024)}, /*index=5*/f32[768]{0:T(1024)}, f32[768]{0:T(1024)}, f32[768]{0:T(1024)}) all-reduce(f32[576]{0:T(1024)S(1)} %reduce_sum.223, f32[768]{0:T(1024)S(1)} %get-tuple-element.36, ...), channel_id=1, replica_groups=mesh['dp'=8,'tensor'=4] {'dp'}, use_global_device_ids=true, to_apply=%region_19.20 | all-reduce | flops 5952 | bytes 47616 | tf_op jit(solution)/shard_map/psum | solution.py:201
  910.5 114.6 %all-reduce.8.cloned.1.call-done = (f32[768,576]{0,1:T(8,128)}, f32[192,768]{1,0:T(8,128)}, f32[768,768]{1,0:T(8,128)}, f32[768,768]{1,0:T(8,128)}) async-done(((f32[768,576]{0,1:T(8,128)}, f32[192,768]{1,0:T(8,128)}, f32[768,768]{1,0:T(8,128)}, f32[768,768]{1,0:T(8,128)}), (f32[768,576]{0,1:T(8,128)}, f32[192,768]{1,0:T(8,128)}, f32[768,768]{1,0:T(8,128)}, ...) | async-done | bytes 7077904 | tf_op jit(solution)/shard_map/psum | solution.py:201
  (289 shorter events, 170.6 us)
Async XLA Ops:
  7.2 337.1 %copy-start = (bf16[768,768]{1,0:T(8,128)(2,1)S(1)}, bf16[768,768]{1,0:T(8,128)(2,1)}, u32[]{:S(2)}) copy-start(bf16[768,768]{1,0:T(8,128)(2,1)} %param.23) | copy-start | bytes 3538948
  7.2 68.6 %all-gather.5.cloned.1.call-start = ((), (), s32[]{:S(2)}) async-start(), calls=%async_computation.4 | async-start | bytes 3932160 | tf_op jit(solution)/shard_map/all_gather | solution.py:142
  7.9 268.9 %reduce-scatter.5.cloned.1.call-start = ((), (), s32[]{:S(2)}) async-start(), calls=%async_computation.5 | async-start | bytes 7864320 | tf_op jit(solution)/shard_map/reduce_scatter | solution.py:145
  12.1 117.7 %copy-start.61 = (s32[32]{0:T(128)}, s32[32]{0:T(128)S(1)}, u32[]{:S(2)}) copy-start(s32[32]{0:T(128)S(1)} %get-tuple-element.20) | copy-start | bytes 388
  12.1 117.7 %copy-start.64 = (s32[32]{0:T(128)}, s32[32]{0:T(128)S(1)}, u32[]{:S(2)}) copy-start(s32[32]{0:T(128)S(1)} %get-tuple-element.21) | copy-start | bytes 388
  12.2 109.0 %copy-start.39 = (f32[32,64]{1,0:T(8,128)}, f32[32,64]{1,0:T(8,128)S(1)}, u32[]{:S(2)}) copy-start(f32[32,64]{1,0:T(8,128)S(1)} %get-tuple-element.63) | copy-start | bytes 24580
  12.3 98.5 %copy-start.44 = (f32[32,64]{1,0:T(8,128)}, f32[32,64]{1,0:T(8,128)S(1)}, u32[]{:S(2)}) copy-start(f32[32,64]{1,0:T(8,128)S(1)} %get-tuple-element.77) | copy-start | bytes 24580
  12.3 98.4 %copy-start.46 = (f32[32,64]{1,0:T(8,128)}, f32[32,64]{1,0:T(8,128)S(1)}, u32[]{:S(2)}) copy-start(f32[32,64]{1,0:T(8,128)S(1)} %get-tuple-element.78) | copy-start | bytes 24580
  12.7 131.7 %copy-start.11 = (f32[32,64,64]{1,2,0:T(8,128)}, f32[32,64,64]{1,2,0:T(8,128)S(1)}, u32[]{:S(2)}) copy-start(f32[32,64,64]{1,2,0:T(8,128)S(1)} %and_convert_fusion) | copy-start | bytes 1572868
  167.2 109.6 %copy-start.27 = (bf16[512,768]{1,0:T(8,128)(2,1)S(1)}, bf16[512,768]{1,0:T(8,128)(2,1)}, u32[]{:S(2)}) copy-start(bf16[512,768]{1,0:T(8,128)(2,1)} %param.15) | copy-start | bytes 2359300
  167.2 177.1 %all-gather.7.cloned.1.call-start = ((), (), s32[]{:S(2)}) async-start(), calls=%async_computation.6 | async-start | bytes 3932160 | tf_op jit(solution)/shard_map/all_gather | solution.py:150
  278.5 74.1 %copy-start.50 = (f32[512]{0:T(512)}, f32[512]{0:T(512)S(1)}, u32[]{:S(2)}) copy-start(f32[512]{0:T(512)S(1)} %broadcast_multiply_fusion.1) | copy-start | bytes 6148
  278.8 73.8 %copy-start.57 = (f32[512]{0:T(512)}, f32[512]{0:T(512)S(1)}, u32[]{:S(2)}) copy-start(f32[512]{0:T(512)S(1)} %multiply_reduce_fusion.5) | copy-start | bytes 6148
  280.1 188.3 %reduce-scatter.7.cloned.1.call-start = ((), (), s32[]{:S(2)}) async-start(), calls=%async_computation.7 | async-start | bytes 7864320 | tf_op jit(solution)/shard_map/reduce_scatter | solution.py:153
  358.8 181.8 %all-gather.9.cloned.1.call-start = ((), (), s32[]{:S(2)}) async-start(), calls=%async_computation.8 | async-start | bytes 3932160 | tf_op jit(solution)/shard_map/all_gather | solution.py:164
  361.3 109.5 %copy-start.26 = (bf16[512,768]{1,0:T(8,128)(2,1)S(1)}, bf16[512,768]{1,0:T(8,128)(2,1)}, u32[]{:S(2)}) copy-start(bf16[512,768]{1,0:T(8,128)(2,1)} %param.29) | copy-start | bytes 2359300
  476.4 189.7 %reduce-scatter.9.cloned.1.call-start = ((), (), s32[]{:S(2)}) async-start(), calls=%async_computation.9 | async-start | bytes 7864320 | tf_op jit(solution)/shard_map/reduce_scatter | solution.py:174
  556.5 109.6 %copy-start.49 = (f32[768]{0:T(1024)S(1)}, f32[768]{0:T(1024)}, u32[]{:S(2)}) copy-start(f32[768]{0:T(1024)} %convert_element_type.155) | copy-start | bytes 9220
  556.5 109.6 %copy-start.51 = (f32[512]{0:T(512)S(1)}, f32[512]{0:T(512)}, u32[]{:S(2)}) copy-start(f32[512]{0:T(512)} %copy-done.50) | copy-start | bytes 6148
  556.5 109.6 %copy-start.54 = (f32[512]{0:T(512)S(1)}, f32[512]{0:T(512)}, u32[]{:S(2)}) copy-start(f32[512]{0:T(512)} %copy-done.53) | copy-start | bytes 6148
  556.6 112.9 %copy-start.58 = (f32[512]{0:T(512)S(1)}, f32[512]{0:T(512)}, u32[]{:S(2)}) copy-start(f32[512]{0:T(512)} %copy-done.57) | copy-start | bytes 6148
  556.6 180.5 %all-gather.11.cloned.1.call-start = ((), (), s32[]{:S(2)}) async-start(), calls=%async_computation.10 | async-start | bytes 3932160 | tf_op jit(solution)/shard_map/all_gather | solution.py:181
  672.9 235.2 %reduce-scatter.11.cloned.1.call-start = ((), (), s32[]{:S(2)}) async-start(), calls=%async_computation.11 | async-start | bytes 3932160 | tf_op jit(solution)/shard_map/reduce_scatter | solution.py:193
  846.6 178.4 %all-reduce.8.cloned.1.call-start = ((), (), s32[]{:S(2)}) async-start(), calls=%async_computation.12 | async-start | bytes 14155776 | tf_op jit(solution)/shard_map/psum | solution.py:201
  (76 other events, 815.8 us)
Sparse Core Ops, SparseCore 0:
  9.6 66.1 all-gather.4
  167.4 109.3 reduce-scatter.4
  280.2 64.0 all-gather.6
  359.0 109.3 reduce-scatter.6
  476.5 64.0 all-gather.8
  556.7 109.3 reduce-scatter.8
  673.1 64.0 all-gather.10
  846.7 59.9 reduce-scatter.10
  911.5 113.4 all-reduce.7
